TPU v7x, 256 devices: a whole 4x4x8 slice. The times are simulated.
256 devices in a mesh: dp: 32 (over z, x), mp: 8 (over y, core).
Axes of the slice: x: 4, y: 4, z: 8, core: 2. Of those that a mesh axis runs over, the one named last changes fastest.
Arguments:
- tokens: bfloat16 [32768, 8192], P('dp', 'mp'), may hold values from -6 to 6
- value_weight: bfloat16 [8192, 1024], P('mp'), may hold values from -0.0625 to 0.0625
- adapter_down_panels: bfloat16 [96, 64, 8192], P('dp', None, 'mp'), may hold values from -0.0625 to 0.0625
- adapter_up_panels: bfloat16 [96, 64, 1024], P('dp', None, 'mp'), may hold values from -0.75 to 0.75
- cotangent: bfloat16 [32768, 1024], P('dp', 'mp'), may hold values from -6 to 6
- block_list_entry: int32 [1024], P('dp'), may hold values from 0 to 31, as said below
- device_tenant_list: int32 [1024], P('dp'), may hold values from 0 to 95, as said below
- tenant_location_map: int32 [96], replicated, may hold values from 0 to 95, as said below
Outputs:
- values: bfloat16 [32768, 1024], P('dp', 'mp')
- token_gradient: bfloat16 [32768, 8192], P('dp', 'mp')
- grad_a: bfloat16 [96, 64, 8192], P('dp', None, 'mp')
- grad_b: bfloat16 [96, 64, 1024], P('dp', None, 'mp')
Inputs may be any that keep to these rules, and one draw needn't show every extreme that they name: `device_tenant_list`: each entry names a tenant; no tenant stands twice in one list. Of one device's 32 entries, at most 2 name tenants whose storage location tenant_location_map[t] lies on one dp index (tenant_location_map[t] // 3), and every device's list has 2 entries on some one dp index. A permutation: tenant t's panels are row tenant_location_map[t] of adapter_down_panels and adapter_up_panels. `block_list_entry`: every entry of a device's tenant list is named by at least one of that device's row blocks.
All inputs are finite; a program needn't handle non-finite values.
Results may differ from a plain program's by a relative error of at most 0.0057.
Values may be sent and summed in bfloat16 or wider, within the bound.
A program may use at most 128 MiB of HBM per device.

v0:
```python
import jax
import jax.numpy as jnp
import numpy as np
from jax import lax
from jax.sharding import Mesh
from jax.sharding import PartitionSpec as P

MOST = 2
DP = ("dz", "dx")


def earlier_same(group):
    count = group.shape[-1]
    ids = jnp.arange(count, dtype=jnp.int32)
    same = (group[..., :, None] == group[..., None, :]) & (ids[:, None] > ids[None, :])
    return jnp.sum(same.astype(jnp.int32), axis=-1)


def shards(
    tokens,
    value_weight,
    adapter_down_panels,
    adapter_up_panels,
    cotangent,
    block_list_entry,
    device_tenant_list,
    tenant_location_map,
):
    rows, width_loc = tokens.shape
    stored, rank, _ = adapter_down_panels.shape
    out_loc = adapter_up_panels.shape[2]
    blocks = block_list_entry.shape[0]
    blk = rows // blocks
    n_z = lax.axis_size("dz")
    n_x = lax.axis_size("dx")
    per_x = min(MOST * n_z, blocks)
    capacity = n_x * per_x
    my_x = lax.axis_index("dx")
    column = n_z * stored
    tenant = jnp.take(device_tenant_list, block_list_entry, mode="clip")
    location = jnp.take(tenant_location_map, tenant, mode="clip")
    owner_x = location // stored % n_x
    position = owner_x * per_x + earlier_same(owner_x)
    slot_ids = jnp.arange(capacity, dtype=jnp.int32)
    block_ids = jnp.arange(blocks, dtype=jnp.int32)
    source = jnp.sum(
        jnp.where(position[None, :] == slot_ids[:, None], block_ids[None, :], 0), axis=1
    )
    x_location = lax.all_gather(location, "dx", axis=0, tiled=False)
    x_owner_x = x_location // stored % n_x
    x_rank = earlier_same(x_owner_x)
    in_column = x_location // stored // n_x * stored + x_location % stored
    mine = x_owner_x == my_x
    slot_panel = (
        jnp.stack(
            [
                jnp.sum(jnp.where(mine & (x_rank == c), in_column + 1, 0), axis=1)
                for c in range(per_x)
            ],
            axis=1,
        ).reshape(capacity)
        - 1
    )
    pick = slot_panel[:, None] == jnp.arange(column, dtype=jnp.int32)[None, :]
    down_col = lax.all_gather(adapter_down_panels, "dz", axis=0, tiled=True)
    up_col = lax.all_gather(adapter_up_panels, "dz", axis=0, tiled=True)
    base_t = lax.psum_scatter(
        lax.dot_general(
            value_weight, tokens, (((0,), (1,)), ((), ())), preferred_element_type=jnp.float32
        ),
        "mp",
        scatter_dimension=0,
        tiled=True,
    )
    cot_full = lax.all_gather(cotangent, "mp", axis=1, tiled=True)
    base_bwd = lax.dot_general(
        cot_full, value_weight, (((1,), (1,)), ((), ())), preferred_element_type=jnp.float32
    )
    token_blocks = tokens.reshape(blocks, blk, width_loc)
    cot_blocks = cotangent.reshape(blocks, blk, out_loc)
    send = jnp.concatenate(
        [jnp.take(token_blocks, source, axis=0), jnp.take(cot_blocks, source, axis=0)], axis=2
    )
    recv = lax.all_to_all(send, "dx", split_axis=0, concat_axis=0, tiled=True)
    tok_recv = recv[:, :, :width_loc]
    cot_recv = recv[:, :, width_loc:]
    panel_at = jnp.clip(slot_panel, 0, column - 1)
    down_sel = jnp.take(down_col, panel_at, axis=0)
    up_sel = jnp.take(up_col, panel_at, axis=0)
    down_part = jnp.einsum("snd,srd->snr", tok_recv, down_sel, preferred_element_type=jnp.float32)
    up_part = jnp.einsum("snc,src->snr", cot_recv, up_sel, preferred_element_type=jnp.float32)
    both = lax.all_gather(
        lax.psum_scatter(
            jnp.stack([down_part, up_part]), "mp", scatter_dimension=1, tiled=True
        ).astype(jnp.bfloat16),
        "mp",
        axis=1,
        tiled=True,
    )
    down_low = both[0]
    up_grad = both[1]
    adapter_out = jnp.einsum("snr,src->snc", down_low, up_sel, preferred_element_type=jnp.float32)
    adapter_bwd = jnp.einsum("snr,srd->snd", up_grad, down_sel, preferred_element_type=jnp.float32)
    back_send = jnp.concatenate(
        [adapter_bwd.astype(jnp.bfloat16), adapter_out.astype(jnp.bfloat16)], axis=2
    )
    back = lax.all_to_all(back_send, "dx", split_axis=0, concat_axis=0, tiled=True)
    pick_rows = jnp.broadcast_to(pick[:, None, :, None], (capacity, blk, column, rank)).reshape(
        capacity * blk, column * rank
    )

    def spread(small):
        wide = jnp.broadcast_to(
            small.reshape(capacity * blk, 1, rank), (capacity * blk, column, rank)
        )
        wide = wide.reshape(capacity * blk, column * rank)
        return jnp.where(pick_rows, wide, jnp.zeros_like(wide))

    grad_a_col = lax.dot_general(
        spread(up_grad),
        tok_recv.reshape(capacity * blk, width_loc),
        (((0,), (0,)), ((), ())),
        preferred_element_type=jnp.float32,
    )
    grad_b_col = lax.dot_general(
        spread(down_low),
        cot_recv.reshape(capacity * blk, out_loc),
        (((0,), (0,)), ((), ())),
        preferred_element_type=jnp.float32,
    )
    grad_a = lax.psum_scatter(grad_a_col, "dz", scatter_dimension=0, tiled=True)
    grad_b = lax.psum_scatter(grad_b_col, "dz", scatter_dimension=0, tiled=True)
    grad_a = grad_a.astype(jnp.bfloat16).reshape(stored, rank, width_loc)
    grad_b = grad_b.astype(jnp.bfloat16).reshape(stored, rank, out_loc)
    mine_back = jnp.take(back, position, axis=0).reshape(rows, width_loc + out_loc)
    values = (base_t.T + mine_back[:, width_loc:].astype(jnp.float32)).astype(jnp.bfloat16)
    token_gradient = (base_bwd + mine_back[:, :width_loc].astype(jnp.float32)).astype(jnp.bfloat16)
    return (values, token_gradient, grad_a, grad_b)


def split_dp(mesh):
    devices = np.asarray(mesh.devices)
    n_dp, n_mp = devices.shape
    try:
        n_x = len({tuple(d.coords)[0] for d in devices[:, 0]})
    except (AttributeError, TypeError):
        n_x = 1
    if n_x < 1 or n_dp % n_x:
        n_x = 1
    return Mesh(devices.reshape(n_dp // n_x, n_x, n_mp), ("dz", "dx", "mp"))


def solution(mesh):
    in_specs = (
        P(DP, "mp"),
        P("mp", None),
        P(DP, None, "mp"),
        P(DP, None, "mp"),
        P(DP, "mp"),
        P(DP),
        P(DP),
        P(),
    )
    out_specs = (P(DP, "mp"), P(DP, "mp"), P(DP, None, "mp"), P(DP, None, "mp"))
    return jax.shard_map(
        shards, mesh=split_dp(mesh), in_specs=in_specs, out_specs=out_specs, check_vma=False
    )
```

profile of v0, /device:TPU:1, one launch (start us, length us, event | category | flops | bytes accessed | tf_op | source)
XLA Modules:
  0.0 417.1 jit_solution(15197474575198803912)
XLA Ops:
  22.0 5.1 %all-to-all-start = ((bf16[64,32,1152]{2,1,0:T(8,128)(2,1)}), bf16[64,32,1152]{2,1,0:T(8,128)(2,1)}, u32[]{:S(2)}, u32[]{:S(2)}) async-start(bf16[64,32,1152]{2,1,0:T(8,128)(2,1)} %pad_maximum_fusion), calls=%async_computation.1 | async-start | bytes 9437184 | tf_op jit(solution)/shard_map/all_to_all | solution.py:84
  28.8 53.5 %all-reduce = s32[128]{0:T(128)S(1)} all-reduce(s32[128]{0:T(128)S(1)} %dynamic-update-slice), channel_id=2, replica_groups=mesh['dz'=8,'dx'=4,'mp'=8] {'dx'}, use_global_device_ids=true, to_apply=%add | all-reduce | flops 128 | bytes 1024
  85.0 24.2 %all_gather.18 = bf16[24,64,128]{2,1,0:T(8,128)(2,1)S(1)} all-gather(bf16[3,64,128]{2,1,0:T(8,128)(2,1)S(1)} %copy-done.5), channel_id=1, replica_groups=mesh['dz'=8,'dx'=4,'mp'=8] {'dz'}, dimensions={0}, use_global_device_ids=true | all-gather | bytes 442368 | tf_op jit(solution)/shard_map/all_gather | solution.py:66
  112.7 7.3 %gather_fusion.4 = bf16[64,64,1024]{2,1,0:T(8,128)(2,1)} fusion(bf16[24,64,1024]{2,1,0:T(8,128)(2,1)} %all-gather.4.cloned.1.call-done, s32[1024]{0:T(1024)S(1)} %pad_clamp_fusion.1), kind=kCustom, calls=%fused_computation.4 | custom fusion | bytes 16777472 | tf_op jit(solution)/shard_map/jit(_take)/gather | solution.py:88
  120.0 7.1 %fusion.3 = f32[1,64,32,64]{3,2,1,0:T(8,128)S(1)} fusion(bf16[64,64,1024]{2,1,0:T(8,128)(2,1)} %gather_fusion.4, pred[64]{0:T(512)(128)(4,1)S(1)} %compare_and_fusion, bf16[64,32,1152]{2,1,0:T(8,128)(2,1)} %all-to-all-done), kind=kOutput, calls=%fused_computation.20 | convolution fusion | flops 272629760 | bytes 13107264 | tf_op jit(solution)/shard_map/snd,srd->snr/dot_general | solution.py:90
  128.7 2.9 reshape.353
  133.6 34.9 %reduce-scatter.13.cloned.1.call-done = f32[8,4096]{1,0:T(8,128)} async-done(((f32[64,4096]{1,0:T(8,128)}), f32[8,4096]{1,0:T(8,128)}) %reduce-scatter.13.cloned.1.call-update) | async-done | bytes 131088
  169.7 17.0 %all_gather.19 = bf16[2,64,32,64]{3,2,1,0:T(8,128)(2,1)S(1)} all-gather(bf16[2,8,32,64]{3,2,1,0:T(8,128)(2,1)S(1)} %copy.69), channel_id=1, replica_groups=mesh['dz'=8,'dx'=4,'mp'=8] {'mp'}, dimensions={1}, use_global_device_ids=true | all-gather | bytes 589824 | tf_op jit(solution)/shard_map/all_gather | solution.py:92
  187.7 9.4 %broadcast_select_fusion = (bf16[64,32,24,64]{3,2,1,0:T(8,128)(2,1)}, bf16[64,32,24,64]{3,2,1,0:T(8,128)(2,1)}) fusion(pred[64,24]{1,0:T(8,128)(4,1)S(1)} %iota_compare_fusion, bf16[64,32,64]{2,1,0:T(8,128)(2,1)S(1)} %get-tuple-element.42, bf16[64,32,64]{2,1,0:T(8,128)(2,1)S(1)} %get-tuple-element.43), kind=kLoop, calls=%fused_computation.7 | loop fusion | flops 6291456 | bytes 13108736 | tf_op jit(solution)/shard_map/jit(_where)/select_n | solution.py:117
  197.1 16.8 %select_n.261 = bf16[2048,1536]{1,0:T(8,128)(2,1)} reshape(bf16[64,32,24,64]{3,2,1,0:T(8,128)(2,1)} %get-tuple-element.44) | data formatting | bytes 12582912 | tf_op jit(solution)/shard_map/jit(_where)/select_n | solution.py:117
  213.9 5.6 %fusion.24 = f32[1536,128]{1,0:T(8,128)} fusion(bf16[2048,1536]{1,0:T(8,128)(2,1)} %select_n.261, bf16[2048,128]{1,0:T(8,128)(2,1)} %bitcast.82), kind=kOutput, calls=%fused_computation.112 | convolution fusion | flops 805306368 | bytes 7602176 | tf_op jit(solution)/shard_map/dot_general | solution.py:125
  220.1 6.0 %fusion.22 = f32[1024,1024]{1,0:T(8,128)} fusion(bf16[1024,1024]{1,0:T(8,128)(2,1)} %param.9, bf16[1024,1024]{1,0:T(8,128)(2,1)S(1)} %copy-done), kind=kOutput, calls=%fused_computation.110 | convolution fusion | flops 2147483648 | bytes 8388608 | tf_op jit(solution)/shard_map/dot_general | solution.py:68
  226.4 5.0 %slice.38 = bf16[64,32,1024]{2,1,0:T(8,128)(2,1)} slice(bf16[64,32,1152]{2,1,0:T(8,128)(2,1)} %all-to-all-done), slice={[0:64], [0:32], [0:1024]} | slice | bytes 8388608 | tf_op jit(solution)/shard_map/slice | solution.py:85
  231.5 16.9 %select_n.259 = bf16[2048,1536]{1,0:T(8,128)(2,1)} reshape(bf16[64,32,24,64]{3,2,1,0:T(8,128)(2,1)} %get-tuple-element.45) | data formatting | bytes 12582912 | tf_op jit(solution)/shard_map/jit(_where)/select_n | solution.py:117
  248.4 11.8 %fusion.23 = f32[1536,1024]{1,0:T(8,128)} fusion(bf16[2048,1536]{1,0:T(8,128)(2,1)} %select_n.259, bf16[2048,1024]{1,0:T(8,128)(2,1)} %bitcast.80), kind=kOutput, calls=%fused_computation.111 | convolution fusion | flops 6442450944 | bytes 16777216 | tf_op jit(solution)/shard_map/dot_general | solution.py:119
  261.9 4.7 %fusion.2 = bf16[64,32,1024]{2,1,0:T(8,128)(2,1)S(1)} fusion(bf16[64,64,1024]{2,1,0:T(8,128)(2,1)} %gather_fusion.4, pred[64]{0:T(512)(128)(4,1)S(1)} %compare_and_fusion, bf16[2,64,32,64]{3,2,1,0:T(8,128)(2,1)S(1)} %copy-done.3), kind=kOutput, calls=%fused_computation.16 | convolution fusion | flops 274726912 | bytes 13107712 | tf_op jit(solution)/shard_map/snr,srd->snd/dot_general | solution.py:103
  269.5 5.1 %all-to-all-start.1 = ((bf16[64,32,1152]{2,1,0:T(8,128)(2,1)}), bf16[64,32,1152]{2,1,0:T(8,128)(2,1)}, u32[]{:S(2)}, u32[]{:S(2)}) async-start(bf16[64,32,1152]{2,1,0:T(8,128)(2,1)} %pad_maximum_fusion.1), calls=%async_computation.2 | async-start | bytes 9437184 | tf_op jit(solution)/shard_map/all_to_all | solution.py:107
  276.3 52.7 %all-to-all-done.1 = bf16[64,32,1152]{2,1,0:T(8,128)(2,1)} async-done(((bf16[64,32,1152]{2,1,0:T(8,128)(2,1)}), bf16[64,32,1152]{2,1,0:T(8,128)(2,1)}, u32[]{:S(2)}, u32[]{:S(2)}) %all-to-all-start.1) | async-done | bytes 4718624 | tf_op jit(solution)/shard_map/all_to_all | solution.py:107
  329.0 4.6 %gather_fusion.6 = bf16[32,32,1152]{2,1,0:T(8,128)(2,1)} fusion(bf16[64,32,1152]{2,1,0:T(8,128)(2,1)} %all-to-all-done.1, s32[1024]{0:T(1024)S(1)} %pad_clamp_fusion), kind=kCustom, calls=%fused_computation.6 | custom fusion | bytes 4718720 | tf_op jit(solution)/shard_map/jit(_take)/gather | solution.py:135
  333.6 4.3 %copy.60 = bf16[1024,1152]{0,1:T(8,128)(2,1)} copy(bf16[1024,1152]{1,0:T(8,128)(2,1)} %bitcast.79) | data formatting | bytes 4718592 | tf_op jit(solution)/shard_map/jit(_take)/gather | solution.py:135
  337.9 3.3 broadcast_select_fusion.8
  341.2 6.7 %add_convert_fusion = bf16[1024,1024]{0,1:T(8,128)(2,1)} fusion(bf16[1024,1152]{0,1:T(8,128)(2,1)} %broadcast_select_fusion.8, bf16[1024,1024]{1,0:T(8,128)(2,1)} %all-gather.6.cloned.1.call-done, bf16[1024,1024]{1,0:T(8,128)(2,1)} %param.9), kind=kOutput, calls=%fused_computation.12 | convolution fusion | flops 2150629376 | bytes 8388608 | tf_op jit(solution)/shard_map/dot_general | solution.py:76
  348.0 3.9 copy.63
  353.9 54.4 %reduce-scatter.9.cloned.1.call-done = f32[192,1024]{1,0:T(8,128)} async-done(((f32[1536,1024]{1,0:T(8,128)}), f32[192,1024]{1,0:T(8,128)}) %reduce-scatter.9.cloned.1.call-update) | async-done | bytes 786448 | tf_op jit(solution)/shard_map/reduce_scatter | solution.py:131
  (106 shorter events, 38.7 us)
Async XLA Ops:
  7.2 6.6 %copy-start = (bf16[1024,1024]{1,0:T(8,128)(2,1)S(1)}, bf16[1024,1024]{1,0:T(8,128)(2,1)}, u32[]{:S(2)}) copy-start(bf16[1024,1024]{1,0:T(8,128)(2,1)} %param.8) | copy-start | bytes 6291460
  7.2 105.5 %all-gather.4.cloned.1.call-start = ((), (), s32[]{:S(2)}) async-start(), calls=%async_computation.7 | async-start | bytes 3538944 | tf_op jit(solution)/shard_map/all_gather | solution.py:65
  11.3 17.2 %copy-start.6 = (s32[32]{0:T(128)}, s32[32]{0:T(128)S(1)}, u32[]{:S(2)}) copy-start(s32[32]{0:T(128)S(1)} %gather_fusion.1) | copy-start | bytes 388
  22.0 5.2 %copy-start.9 = (u32[256]{0:T(256)S(1)}, u32[256]{0:T(256)}, u32[]{:S(2)}) copy-start(u32[256]{0:T(256)} %constant.169) | copy-start | bytes 3076
  22.0 62.9 %copy-start.5 = (bf16[3,64,128]{2,1,0:T(8,128)(2,1)S(1)}, bf16[3,64,128]{2,1,0:T(8,128)(2,1)}, u32[]{:S(2)}) copy-start(bf16[3,64,128]{2,1,0:T(8,128)(2,1)} %param.11) | copy-start | bytes 147460
  22.0 87.9 %all-to-all-start = ((bf16[64,32,1152]{2,1,0:T(8,128)(2,1)}), bf16[64,32,1152]{2,1,0:T(8,128)(2,1)}, u32[]{:S(2)}, u32[]{:S(2)}) async-start(bf16[64,32,1152]{2,1,0:T(8,128)(2,1)} %pad_maximum_fusion), calls=%async_computation.1 | async-start | bytes 9437184 | tf_op jit(solution)/shard_map/all_to_all | solution.py:84
  27.2 141.4 %reduce-scatter.13.cloned.1.call-start = ((), (), s32[]{:S(2)}) async-start(), calls=%async_computation.11 | async-start | bytes 1179648
  120.0 7.1 %copy-start.4 = (f32[1,64,32,64]{3,2,1,0:T(8,128)S(1)}, f32[1,64,32,64]{3,2,1,0:T(8,128)}, u32[]{:S(2)}) copy-start(f32[1,64,32,64]{3,2,1,0:T(8,128)} %convolution_bitcast_fusion) | copy-start | bytes 1572868
  131.6 143.2 %reduce-scatter.11.cloned.1.call-start = ((), (), s32[]{:S(2)}) async-start(), calls=%async_computation.10 | async-start | bytes 884736 | tf_op jit(solution)/shard_map/reduce_scatter | solution.py:132
  186.6 1.0 copy-start.2
  219.5 121.7 %all-gather.6.cloned.1.call-start = ((), (), s32[]{:S(2)}) async-start(), calls=%async_computation.8 | async-start | bytes 2359296 | tf_op jit(solution)/shard_map/all_gather | solution.py:75
  220.1 131.8 %reduce-scatter.7.cloned.1.call-start = ((), (), s32[]{:S(2)}) async-start(), calls=%async_computation.6 | async-start | bytes 4718592 | tf_op jit(solution)/shard_map/reduce_scatter | solution.py:67
  226.2 182.2 %reduce-scatter.9.cloned.1.call-start = ((), (), s32[]{:S(2)}) async-start(), calls=%async_computation.9 | async-start | bytes 7077888 | tf_op jit(solution)/shard_map/reduce_scatter | solution.py:131
  260.2 1.2 copy-start.3
  269.5 5.3 %copy-start.7 = (s32[32]{0:T(128)S(1)}, s32[32]{0:T(128)}, u32[]{:S(2)}) copy-start(s32[32]{0:T(128)} %copy-done.6) | copy-start | bytes 388
  269.5 5.3 %copy-start.8 = (s32[32]{0:T(128)S(1)}, s32[32]{0:T(128)}, u32[]{:S(2)}) copy-start(s32[32]{0:T(128)} %get-tuple-element.39) | copy-start | bytes 388
  269.5 59.5 %all-to-all-start.1 = ((bf16[64,32,1152]{2,1,0:T(8,128)(2,1)}), bf16[64,32,1152]{2,1,0:T(8,128)(2,1)}, u32[]{:S(2)}, u32[]{:S(2)}) async-start(bf16[64,32,1152]{2,1,0:T(8,128)(2,1)} %pad_maximum_fusion.1), calls=%async_computation.2 | async-start | bytes 9437184 | tf_op jit(solution)/shard_map/all_to_all | solution.py:107
  341.2 69.0 %copy-start.1 = (bf16[1024,1024]{1,0:T(8,128)(2,1)S(1)}, bf16[1024,1024]{1,0:T(8,128)(2,1)}, u32[]{:S(2)}) copy-start(bf16[1024,1024]{1,0:T(8,128)(2,1)} %param.8) | copy-start | bytes 6291460
Sparse Core Ops, SparseCore 0:
  9.8 48.5 all-gather.3
  131.7 36.7 reduce-scatter.12
  219.6 32.7 reduce-scatter.10
  254.3 33.2 all-gather.5
  290.1 39.1 reduce-scatter.6
  331.9 76.4 reduce-scatter.8
where the time goes:
time: 419 us; the launch traced here: 417 us
  waiting for transfers between devices  143 us (34%)
  blocking collectives  94.7 us (23%)
  local copies, waits for them, and re-layouts  78.8 us (19%)
  matrix products  45.2 us (11%)
  other arithmetic  29.5 us (7%)
  between operations  15 us (4%)
  starting transfers between devices  10.7 us (3%)
    reduce_scatter x1, waiting for transfers between devices, shards(): grad_a = lax.psum_scatter(grad_a_col, 'dz', scatter_dimension=0, tiled=True)  54.4 us
    unnamed x1, blocking collectives  53.5 us
    all_to_all x1, waiting for transfers between devices, shards(): lax.all_to_all(back_send, 'dx', split_axis=0, concat_axis=0, tiled=True)  52.7 us
    unnamed x7, waiting for transfers between devices  36.2 us
    select_n x2, local copies, waits for them, and re-layouts, spread(): return jnp.where(pick_rows, wide, jnp.zeros_like(wide))  33.8 us
    all_gather x1, blocking collectives, shards(): up_col = lax.all_gather(adapter_up_panels, 'dz', axis=0, tiled=True)  24.2 us
    all_gather x1, blocking collectives, shards(): lax.all_gather(lax.psum_scatter(jnp.stack([down_part, up_part]), 'mp', sc...  17 us
    dot_general x1, matrix products, shards(): lax.dot_general(spread(up_grad), tok_recv.reshape(capacity * blk, width_l...  11.8 us
  transfers between devices with their start and end apart: 8, of which 3 were waited for; matrix products, arithmetic and copies ran while one was open for 23% of the time, Pallas kernels for 0%

commit v1 on v0

--- a/solution.py
+++ b/solution.py
@@ -63,7 +63,15 @@
     )
     pick = slot_panel[:, None] == jnp.arange(column, dtype=jnp.int32)[None, :]
     down_col = lax.all_gather(adapter_down_panels, "dz", axis=0, tiled=True)
-    up_col = lax.all_gather(adapter_up_panels, "dz", axis=0, tiled=True)
+    up_col = jnp.concatenate(
+        lax.all_to_all(
+            jnp.stack([adapter_up_panels] * lax.axis_size("dz"), axis=0),
+            concat_axis=0,
+            axis_name="dz",
+            split_axis=0,
+        ),
+        axis=0,
+    )
     base_t = lax.psum_scatter(
         lax.dot_general(
             value_weight, tokens, (((0,), (1,)), ((), ())), preferred_element_type=jnp.float32

time: 419 us -> 406 us (0.969)
  blocking collectives: 94.7 us -> 71 us
  starting transfers between devices: 10.7 us -> 19.7 us
  other arithmetic: 29.5 us -> 34.2 us
    all_gather x1 -> x0, blocking collectives: 24.2 us -> none  [shards(): up_col = lax.all_gather(adapter_up_panels, 'dz', axis=0, tiled=True)]
    all_to_all x0 -> x1, starting transfers between devices: none -> 9.01 us  [shards(): lax.all_to_all(jnp.stack([adapter_up_panels] * lax.axis_size('dz'), axis=...]
    unnamed x28 -> x30, local copies, waits for them, and re-layouts: 11.8 us -> 11.8 us
  transfers between devices with their start and end apart: 8 -> 9, of which waited for: 3 -> 3; matrix products, arithmetic and copies ran while one was open for 23% -> 25% of each run, Pallas kernels for 0% -> 0%
where the time goes in v1:
time: 406 us; the launch traced here: 404 us
  waiting for transfers between devices  140 us (34%)
  local copies, waits for them, and re-layouts  79.6 us (20%)
  blocking collectives  71 us (17%)
  matrix products  45.1 us (11%)
  other arithmetic  34.2 us (8%)
  starting transfers between devices  19.7 us (5%)
  between operations  15 us (4%)
    reduce_scatter x1, waiting for transfers between devices, shards(): grad_a = lax.psum_scatter(grad_a_col, 'dz', scatter_dimension=0, tiled=True)  54.5 us
    unnamed x1, blocking collectives  54 us
    all_to_all x1, waiting for transfers between devices, shards(): lax.all_to_all(back_send, 'dx', split_axis=0, concat_axis=0, tiled=True)  52.7 us
    select_n x2, local copies, waits for them, and re-layouts, spread(): return jnp.where(pick_rows, wide, jnp.zeros_like(wide))  33.8 us
    unnamed x7, waiting for transfers between devices  32.6 us
    all_gather x1, blocking collectives, shards(): lax.all_gather(lax.psum_scatter(jnp.stack([down_part, up_part]), 'mp', sc...  17 us
    dot_general x1, matrix products, shards(): lax.dot_general(spread(up_grad), tok_recv.reshape(capacity * blk, width_l...  11.8 us
    unnamed x30, local copies, waits for them, and re-layouts  11.8 us
  transfers between devices with their start and end apart: 9, of which 3 were waited for; matrix products, arithmetic and copies ran while one was open for 25% of the time, Pallas kernels for 0%

profile of v1, /device:TPU:1, one launch (start us, length us, event | category | flops | bytes accessed | tf_op | source)
XLA Modules:
  0.0 404.3 jit_solution(11780823363085790427)
XLA Ops:
  9.6 9.0 %all-to-all-start.1 = ((bf16[8,3,64,128]{3,2,1,0:T(8,128)(2,1)}), bf16[8,3,64,128]{3,2,1,0:T(8,128)(2,1)S(1)}, u32[]{:S(2)}, u32[]{:S(2)}) async-start(bf16[8,3,64,128]{3,2,1,0:T(8,128)(2,1)} %stack.89), calls=%async_computation.2 | async-start | bytes 786432 | tf_op jit(solution)/shard_map/all_to_all | solution.py:67
  25.6 4.7 %broadcast_select_fusion.3 = bf16[64,32,1024]{2,1,0:T(8,128)(2,1)} fusion(bf16[64,32,1024]{2,1,0:T(8,128)(2,1)} %gather_fusion.2, pred[64]{0:T(512)(128)(4,1)S(1)} %compare_and_fusion.1), kind=kLoop, calls=%fused_computation.13 | loop fusion | flops 2097152 | bytes 8388672 | tf_op jit(solution)/shard_map/jit(_take)/select_n | solution.py:90
  31.1 5.0 %pad_maximum_fusion = bf16[64,32,1152]{2,1,0:T(8,128)(2,1)} fusion(bf16[64,32,128]{2,1,0:T(8,128)(2,1)S(1)} %broadcast_select_fusion.12, bf16[64,32,1024]{2,1,0:T(8,128)(2,1)} %broadcast_select_fusion.3), kind=kLoop, calls=%fused_computation.10 | loop fusion | flops 9437184 | bytes 9437184 | tf_op jit(solution)/shard_map/concatenate | solution.py:89
  36.1 5.1 %all-to-all-start = ((bf16[64,32,1152]{2,1,0:T(8,128)(2,1)}), bf16[64,32,1152]{2,1,0:T(8,128)(2,1)}, u32[]{:S(2)}, u32[]{:S(2)}) async-start(bf16[64,32,1152]{2,1,0:T(8,128)(2,1)} %pad_maximum_fusion), calls=%async_computation.1 | async-start | bytes 9437184 | tf_op jit(solution)/shard_map/all_to_all | solution.py:92
  42.8 54.0 %all-reduce = s32[128]{0:T(128)S(1)} all-reduce(s32[128]{0:T(128)S(1)} %dynamic-update-slice), channel_id=2, replica_groups=mesh['dz'=8,'dx'=4,'mp'=8] {'dx'}, use_global_device_ids=true, to_apply=%add | all-reduce | flops 128 | bytes 1024
  103.5 7.3 %gather_fusion.4 = bf16[64,64,1024]{2,1,0:T(8,128)(2,1)} fusion(bf16[24,64,1024]{2,1,0:T(8,128)(2,1)} %all-gather.4.cloned.1.call-done, s32[1024]{0:T(1024)S(1)} %pad_clamp_fusion.1), kind=kCustom, calls=%fused_computation.4 | custom fusion | bytes 16777472 | tf_op jit(solution)/shard_map/jit(_take)/gather | solution.py:96
  110.8 7.1 %fusion.3 = f32[1,64,32,64]{3,2,1,0:T(8,128)S(1)} fusion(bf16[64,64,1024]{2,1,0:T(8,128)(2,1)} %gather_fusion.4, pred[64]{0:T(512)(128)(4,1)S(1)} %copy-done.9, bf16[64,32,1152]{2,1,0:T(8,128)(2,1)} %all-to-all-done), kind=kOutput, calls=%fused_computation.20 | convolution fusion | flops 272629760 | bytes 13107264 | tf_op jit(solution)/shard_map/snd,srd->snr/dot_general | solution.py:98
  124.4 31.3 %reduce-scatter.13.cloned.1.call-done = f32[8,4096]{1,0:T(8,128)} async-done(((f32[64,4096]{1,0:T(8,128)}), f32[8,4096]{1,0:T(8,128)}) %reduce-scatter.13.cloned.1.call-update) | async-done | bytes 131088
  156.9 17.0 %all_gather.15 = bf16[2,64,32,64]{3,2,1,0:T(8,128)(2,1)S(1)} all-gather(bf16[2,8,32,64]{3,2,1,0:T(8,128)(2,1)S(1)} %copy.69), channel_id=1, replica_groups=mesh['dz'=8,'dx'=4,'mp'=8] {'mp'}, dimensions={1}, use_global_device_ids=true | all-gather | bytes 589824 | tf_op jit(solution)/shard_map/all_gather | solution.py:100
  174.9 9.4 %broadcast_select_fusion = (bf16[64,32,24,64]{3,2,1,0:T(8,128)(2,1)}, bf16[64,32,24,64]{3,2,1,0:T(8,128)(2,1)}) fusion(pred[64,24]{1,0:T(8,128)(4,1)S(1)} %iota_compare_fusion, bf16[64,32,64]{2,1,0:T(8,128)(2,1)S(1)} %get-tuple-element.42, bf16[64,32,64]{2,1,0:T(8,128)(2,1)S(1)} %get-tuple-element.43), kind=kLoop, calls=%fused_computation.7 | loop fusion | flops 6291456 | bytes 13108736 | tf_op jit(solution)/shard_map/jit(_where)/select_n | solution.py:125
  184.3 16.8 %select_n.261 = bf16[2048,1536]{1,0:T(8,128)(2,1)} reshape(bf16[64,32,24,64]{3,2,1,0:T(8,128)(2,1)} %get-tuple-element.44) | data formatting | bytes 12582912 | tf_op jit(solution)/shard_map/jit(_where)/select_n | solution.py:125
  201.1 5.6 %fusion.24 = f32[1536,128]{1,0:T(8,128)} fusion(bf16[2048,1536]{1,0:T(8,128)(2,1)} %select_n.261, bf16[2048,128]{1,0:T(8,128)(2,1)} %bitcast.84), kind=kOutput, calls=%fused_computation.112 | convolution fusion | flops 805306368 | bytes 7602176 | tf_op jit(solution)/shard_map/dot_general | solution.py:133
  207.3 6.0 %fusion.22 = f32[1024,1024]{1,0:T(8,128)} fusion(bf16[1024,1024]{1,0:T(8,128)(2,1)} %param.9, bf16[1024,1024]{1,0:T(8,128)(2,1)S(1)} %copy-done), kind=kOutput, calls=%fused_computation.110 | convolution fusion | flops 2147483648 | bytes 8388608 | tf_op jit(solution)/shard_map/dot_general | solution.py:76
  213.6 5.0 %slice.38 = bf16[64,32,1024]{2,1,0:T(8,128)(2,1)} slice(bf16[64,32,1152]{2,1,0:T(8,128)(2,1)} %all-to-all-done), slice={[0:64], [0:32], [0:1024]} | slice | bytes 8388608 | tf_op jit(solution)/shard_map/slice | solution.py:93
  218.7 16.9 %select_n.259 = bf16[2048,1536]{1,0:T(8,128)(2,1)} reshape(bf16[64,32,24,64]{3,2,1,0:T(8,128)(2,1)} %get-tuple-element.45) | data formatting | bytes 12582912 | tf_op jit(solution)/shard_map/jit(_where)/select_n | solution.py:125
  235.6 11.8 %fusion.23 = f32[1536,1024]{1,0:T(8,128)} fusion(bf16[2048,1536]{1,0:T(8,128)(2,1)} %select_n.259, bf16[2048,1024]{1,0:T(8,128)(2,1)} %bitcast.82), kind=kOutput, calls=%fused_computation.111 | convolution fusion | flops 6442450944 | bytes 16777216 | tf_op jit(solution)/shard_map/dot_general | solution.py:127
  249.1 4.7 %fusion.2 = bf16[64,32,1024]{2,1,0:T(8,128)(2,1)S(1)} fusion(bf16[64,64,1024]{2,1,0:T(8,128)(2,1)} %gather_fusion.4, pred[64]{0:T(512)(128)(4,1)S(1)} %copy-done.9, bf16[2,64,32,64]{3,2,1,0:T(8,128)(2,1)S(1)} %copy-done.3), kind=kOutput, calls=%fused_computation.16 | convolution fusion | flops 274726912 | bytes 13107712 | tf_op jit(solution)/shard_map/snr,srd->snd/dot_general | solution.py:111
  256.6 5.1 %all-to-all-start.2 = ((bf16[64,32,1152]{2,1,0:T(8,128)(2,1)}), bf16[64,32,1152]{2,1,0:T(8,128)(2,1)}, u32[]{:S(2)}, u32[]{:S(2)}) async-start(bf16[64,32,1152]{2,1,0:T(8,128)(2,1)} %pad_maximum_fusion.1), calls=%async_computation.3 | async-start | bytes 9437184 | tf_op jit(solution)/shard_map/all_to_all | solution.py:115
  263.5 52.7 %all-to-all-done.2 = bf16[64,32,1152]{2,1,0:T(8,128)(2,1)} async-done(((bf16[64,32,1152]{2,1,0:T(8,128)(2,1)}), bf16[64,32,1152]{2,1,0:T(8,128)(2,1)}, u32[]{:S(2)}, u32[]{:S(2)}) %all-to-all-start.2) | async-done | bytes 4718624 | tf_op jit(solution)/shard_map/all_to_all | solution.py:115
  316.2 4.6 %gather_fusion.6 = bf16[32,32,1152]{2,1,0:T(8,128)(2,1)} fusion(bf16[64,32,1152]{2,1,0:T(8,128)(2,1)} %all-to-all-done.2, s32[1024]{0:T(1024)S(1)} %pad_clamp_fusion), kind=kCustom, calls=%fused_computation.6 | custom fusion | bytes 4718720 | tf_op jit(solution)/shard_map/jit(_take)/gather | solution.py:143
  320.8 4.3 %copy.60 = bf16[1024,1152]{0,1:T(8,128)(2,1)} copy(bf16[1024,1152]{1,0:T(8,128)(2,1)} %bitcast.80) | data formatting | bytes 4718592 | tf_op jit(solution)/shard_map/jit(_take)/gather | solution.py:143
  328.4 6.7 %add_convert_fusion = bf16[1024,1024]{0,1:T(8,128)(2,1)} fusion(bf16[1024,1152]{0,1:T(8,128)(2,1)} %broadcast_select_fusion.8, bf16[1024,1024]{1,0:T(8,128)(2,1)} %all-gather.6.cloned.1.call-done, bf16[1024,1024]{1,0:T(8,128)(2,1)} %param.9), kind=kOutput, calls=%fused_computation.12 | convolution fusion | flops 2150629376 | bytes 8388608 | tf_op jit(solution)/shard_map/dot_general | solution.py:84
  335.1 3.9 copy.63
  341.1 54.5 %reduce-scatter.9.cloned.1.call-done = f32[192,1024]{1,0:T(8,128)} async-done(((f32[1536,1024]{1,0:T(8,128)}), f32[192,1024]{1,0:T(8,128)}) %reduce-scatter.9.cloned.1.call-update) | async-done | bytes 786448 | tf_op jit(solution)/shard_map/reduce_scatter | solution.py:139
  (110 shorter events, 40.8 us)
Async XLA Ops:
  7.2 15.6 %copy-start = (bf16[1024,1024]{1,0:T(8,128)(2,1)S(1)}, bf16[1024,1024]{1,0:T(8,128)(2,1)}, u32[]{:S(2)}) copy-start(bf16[1024,1024]{1,0:T(8,128)(2,1)} %param.8) | copy-start | bytes 6291460
  7.2 96.3 %all-gather.4.cloned.1.call-start = ((), (), s32[]{:S(2)}) async-start(), calls=%async_computation.8 | async-start | bytes 3538944 | tf_op jit(solution)/shard_map/all_gather | solution.py:65
  9.6 26.5 %all-to-all-start.1 = ((bf16[8,3,64,128]{3,2,1,0:T(8,128)(2,1)}), bf16[8,3,64,128]{3,2,1,0:T(8,128)(2,1)S(1)}, u32[]{:S(2)}, u32[]{:S(2)}) async-start(bf16[8,3,64,128]{3,2,1,0:T(8,128)(2,1)} %stack.89), calls=%async_computation.2 | async-start | bytes 786432 | tf_op jit(solution)/shard_map/all_to_all | solution.py:67
  21.9 20.6 %copy-start.6 = (s32[32]{0:T(128)}, s32[32]{0:T(128)S(1)}, u32[]{:S(2)}) copy-start(s32[32]{0:T(128)S(1)} %gather_fusion.1) | copy-start | bytes 388
  25.6 4.7 %copy-start.5 = (bf16[1024,128]{1,0:T(8,128)(2,1)S(1)}, bf16[1024,128]{1,0:T(8,128)(2,1)}, u32[]{:S(2)}) copy-start(bf16[1024,128]{1,0:T(8,128)(2,1)} %param.12) | copy-start | bytes 786436
  36.1 5.2 %copy-start.10 = (u32[256]{0:T(256)S(1)}, u32[256]{0:T(256)}, u32[]{:S(2)}) copy-start(u32[256]{0:T(256)} %constant.169) | copy-start | bytes 3076
  36.1 64.7 %all-to-all-start = ((bf16[64,32,1152]{2,1,0:T(8,128)(2,1)}), bf16[64,32,1152]{2,1,0:T(8,128)(2,1)}, u32[]{:S(2)}, u32[]{:S(2)}) async-start(bf16[64,32,1152]{2,1,0:T(8,128)(2,1)} %pad_maximum_fusion), calls=%async_computation.1 | async-start | bytes 9437184 | tf_op jit(solution)/shard_map/all_to_all | solution.py:92
  41.2 114.6 %reduce-scatter.13.cloned.1.call-start = ((), (), s32[]{:S(2)}) async-start(), calls=%async_computation.12 | async-start | bytes 1179648
  103.5 7.3 %copy-start.9 = (pred[64]{0:T(512)(128)(4,1)S(1)}, pred[64]{0:T(512)(128)(4,1)}, u32[]{:S(2)}) copy-start(pred[64]{0:T(512)(128)(4,1)} %compare_and_fusion) | copy-start | bytes 196
  110.8 7.1 %copy-start.4 = (f32[1,64,32,64]{3,2,1,0:T(8,128)S(1)}, f32[1,64,32,64]{3,2,1,0:T(8,128)}, u32[]{:S(2)}) copy-start(f32[1,64,32,64]{3,2,1,0:T(8,128)} %convolution_bitcast_fusion) | copy-start | bytes 1572868
  122.4 139.5 %reduce-scatter.11.cloned.1.call-start = ((), (), s32[]{:S(2)}) async-start(), calls=%async_computation.11 | async-start | bytes 884736 | tf_op jit(solution)/shard_map/reduce_scatter | solution.py:140
  173.8 1.0 copy-start.2
  206.7 121.7 %all-gather.6.cloned.1.call-start = ((), (), s32[]{:S(2)}) async-start(), calls=%async_computation.9 | async-start | bytes 2359296 | tf_op jit(solution)/shard_map/all_gather | solution.py:83
  207.3 131.8 %reduce-scatter.7.cloned.1.call-start = ((), (), s32[]{:S(2)}) async-start(), calls=%async_computation.7 | async-start | bytes 4718592 | tf_op jit(solution)/shard_map/reduce_scatter | solution.py:75
  213.3 182.2 %reduce-scatter.9.cloned.1.call-start = ((), (), s32[]{:S(2)}) async-start(), calls=%async_computation.10 | async-start | bytes 7077888 | tf_op jit(solution)/shard_map/reduce_scatter | solution.py:139
  247.4 1.2 copy-start.3
  256.6 5.3 %copy-start.7 = (s32[32]{0:T(128)S(1)}, s32[32]{0:T(128)}, u32[]{:S(2)}) copy-start(s32[32]{0:T(128)} %copy-done.6) | copy-start | bytes 388
  256.6 5.3 %copy-start.8 = (s32[32]{0:T(128)S(1)}, s32[32]{0:T(128)}, u32[]{:S(2)}) copy-start(s32[32]{0:T(128)} %get-tuple-element.39) | copy-start | bytes 388
  256.6 59.5 %all-to-all-start.2 = ((bf16[64,32,1152]{2,1,0:T(8,128)(2,1)}), bf16[64,32,1152]{2,1,0:T(8,128)(2,1)}, u32[]{:S(2)}, u32[]{:S(2)}) async-start(bf16[64,32,1152]{2,1,0:T(8,128)(2,1)} %pad_maximum_fusion.1), calls=%async_computation.3 | async-start | bytes 9437184 | tf_op jit(solution)/shard_map/all_to_all | solution.py:115
  328.4 69.1 %copy-start.1 = (bf16[1024,1024]{1,0:T(8,128)(2,1)S(1)}, bf16[1024,1024]{1,0:T(8,128)(2,1)}, u32[]{:S(2)}) copy-start(bf16[1024,1024]{1,0:T(8,128)(2,1)} %param.8) | copy-start | bytes 6291460
Sparse Core Ops, SparseCore 0:
  9.8 50.7 all-gather.3
  122.5 33.1 reduce-scatter.12
  206.8 32.8 reduce-scatter.10
  241.5 33.2 all-gather.5
  277.3 39.1 reduce-scatter.6
  319.1 76.4 reduce-scatter.8
